TPU v7x, 32 devices: a whole 2x2x4 slice. The times are simulated.
32 devices in a mesh: band: 32 (over z, y, x, core).
Axes of the slice: x: 2, y: 2, z: 4, core: 2. Of those that a mesh axis runs over, the one named last changes fastest.
Arguments:
- rho_low: float32 [2, 32, 128, 128], replicated, may hold values from -6 to 6
- kprev_low: float32 [2, 32, 128, 128], replicated, may hold values from -6 to 6
- rho_band: float32 [2, 512, 128, 128], P(None, 'band'), may hold values from -6 to 6
- kprev_band: float32 [2, 512, 128, 128], P(None, 'band'), may hold values from -6 to 6
- hamiltonian: float32 [2, 128, 128], replicated, as said below
- state_site: int32 [128], replicated, may hold values from 0 to 23
- coupling_mag: float32 [72], replicated, may hold values from 0.2 to 2
- coupling_phase: float32 [72], replicated, may hold values from -3.140625 to 3.140625
- damping_rate: float32 [72], replicated, may hold values from 0.05 to 2
- low_mode: int32 [31], replicated, may hold values from 0 to 71, as said below
- occupation: int32 [512, 72], P('band'), may hold values from 0 to 3, as said below
- couple_src: int32 [512, 16], P('band'), may hold values from -1 to 543, as said below
- couple_mode: int32 [512, 16], P('band'), may hold values from 0 to 71, as said below
- couple_dir: int32 [512, 16], P('band'), may hold values from 0 to 1
Outputs:
- k_low: float32 [2, 32, 128, 128], replicated
- k_band: float32 [2, 512, 128, 128], P(None, 'band')
Inputs may be any that keep to these rules, and one draw needn't show every extreme that they name: `hamiltonian`: the real part is symmetric and the imaginary part antisymmetric (a Hermitian matrix). `low_mode`: distinct modes. `occupation`: each operator has one to three quanta in all. `couple_src`: all couplings of one device's operators to operators held by one other device read one and the same operator of that device. A low-tier source is never 0, and couplings to low-tier sources have direction 1. Each device's far couplings reach devices spread over the whole axis. `couple_mode`: for direction 1 the mode is occupied in the destination operator.
All inputs are finite; a program needn't handle non-finite values.
Results may differ from a plain program's by a relative error of at most 0.0003.
Values sent between devices are 32-bit elements; how exact they have to be, the bound alone decides.
No kernel may reach another device: no remote copies, remote signals or barrier semaphores. Data moves between devices by JAX's collectives and lax.ppermute only.
A program may use at most 192 MiB of HBM per device.

v0:
```python
import functools
import math

import jax
import jax.numpy as jnp
from jax import lax
from jax.experimental import pallas as pl
from jax.experimental.pallas import tpu as pltpu
from jax.sharding import PartitionSpec as P


EXPS = 3
OUTER = 4
BLOCKS = (4, 5, 7)
section_weight = 0.2
VMEM_LIMIT = 60 * 1024 * 1024

vmem = pl.BlockSpec(memory_space=pltpu.VMEM)
smem = pl.BlockSpec(memory_space=pltpu.SMEM)
hbm = pl.BlockSpec(memory_space=pl.ANY)


def fill_masks(row_ref, diff_ref, sum_ref=None, start=0):
    sites, height, size = diff_ref.shape
    site_b = jnp.broadcast_to(row_ref[...].astype(jnp.float32), (size, size))
    site_a = jnp.transpose(site_b)[start : start + height]
    site_b = site_b[start : start + height]

    def one_site(s, carry):
        s_f = lax.convert_element_type(s, jnp.float32)
        va = jnp.where(site_a == s_f, 1.0, 0.0)
        vb = jnp.where(site_b == s_f, 1.0, 0.0)
        diff_ref[s] = va - vb
        if sum_ref is not None:
            sum_ref[s] = va + vb
        return carry

    lax.fori_loop(0, sites, one_site, 0)


def split(x):
    high = x.astype(jnp.bfloat16)
    return high, (x - high.astype(jnp.float32)).astype(jnp.bfloat16)


def matmul(x, y):
    def dot(a, b):
        return jnp.dot(a, b, preferred_element_type=jnp.float32)

    return dot(x[0], y[0]) + (dot(x[0], y[1]) + dot(x[1], y[0]))


def commutator(h_re, h_im, y_pair):
    size = y_pair.shape[-1]
    left, right = [], []
    for re, im in zip(h_re, h_im):
        top = jnp.concatenate([re, -im], axis=1)
        low = jnp.concatenate([im, re], axis=1)
        left.append(jnp.concatenate([top, low], axis=0))
        top = jnp.concatenate([re, im], axis=1)
        low = jnp.concatenate([-im, re], axis=1)
        right.append(jnp.concatenate([top, low], axis=0))
    lhs = matmul(left, split(y_pair.reshape(2 * size, size)))
    rhs = matmul(split(jnp.concatenate([y_pair[0], y_pair[1]], axis=1)), right)
    return lhs[:size] - rhs[:, :size], lhs[size:] - rhs[:, size:]


LOW_J, LOW_S, NEAR_M, _, FAR_M, _, COUNTS, OWN_I = range(8)
LOW_A, NEAR_A, _, FAR_A, _, DAMP, OWN_F = range(7)


def prep_kernel(
    low_count, own, src, mode, direction, occ, mag, cos, sin, rate, low_mode, ints, flts
):
    rows, width = src.shape
    modes = occ.shape[1]
    others = low_mode.shape[1]
    own_index, band_size, inner = own[0], own[1], own[2]
    outer = band_size // inner
    f32, i32 = jnp.float32, jnp.int32
    lane_mode = lax.broadcasted_iota(i32, (rows, modes), 1)
    lane_low = lax.broadcasted_iota(i32, (rows, others), 1)
    lane_col = lax.broadcasted_iota(i32, (rows, width), 1)
    occ_f = occ[...].astype(f32)
    mag_b = jnp.broadcast_to(mag[...], (rows, modes))
    cos_b = jnp.broadcast_to(cos[...], (rows, modes))
    sin_b = jnp.broadcast_to(sin[...], (rows, modes))
    rate_b = jnp.broadcast_to(rate[...], (rows, modes))
    mark_b = jnp.broadcast_to(low_mode[...].astype(f32) + 1.0, (rows, others))

    def total(x):
        return jnp.sum(x, axis=1, keepdims=True)

    zero_i = jnp.zeros((rows, width), i32)
    zero_f = jnp.zeros((rows, width), f32)
    int_out = [zero_i] * 6
    flt_out = [zero_f] * 5
    fill = [jnp.zeros((rows, 1), i32)] * 3
    for c in range(width):
        src_c, mode_c = src[:, c : c + 1], mode[:, c : c + 1]
        down = direction[:, c : c + 1] == 1
        hit = lane_mode == mode_c
        level = total(jnp.where(hit, occ_f, 0.0))
        strength = total(jnp.where(hit, mag_b, 0.0))
        amp_down = jnp.sqrt(level * strength)
        amp_up = jnp.sqrt((level + 1.0) * strength)
        alpha = jnp.where(down, amp_down * total(jnp.where(hit, cos_b, 0.0)), amp_up)
        beta = jnp.where(down, amp_down * total(jnp.where(hit, sin_b, 0.0)), 0.0)
        mark = total(jnp.where(lane_low == src_c - 1, mark_b, 0.0))
        held = jnp.where(mark == mode_c.astype(f32) + 1.0, 2.0, 1.0)
        alpha_low = jnp.sqrt(held * strength)
        site = mode_c // EXPS
        live = src_c >= 0
        is_low = live & (src_c < low_count)
        shifted = jnp.maximum(src_c - low_count, 0)
        owner = shifted // rows
        local = is_low | (live & (owner == own_index))
        far_m = (owner % inner) * outer + ((owner // inner) ^ (own_index // inner))
        near_m = jnp.where(is_low, src_c, low_count + shifted % rows)
        lists = (
            (is_low, (src_c, site), (alpha_low,)),
            (local, (near_m, site), (alpha, beta)),
            (live & ~local, (far_m, site), (alpha, beta)),
        )
        at_f = 0
        for which, (flag, int_cols, flt_cols) in enumerate(lists):
            put = (lane_col == fill[which]) & flag
            for i, value in enumerate(int_cols):
                int_out[2 * which + i] = int_out[2 * which + i] + jnp.where(put, value, 0)
            for value in flt_cols:
                flt_out[at_f] = flt_out[at_f] + jnp.where(put, value, 0.0)
                at_f += 1
            fill[which] = fill[which] + jnp.where(flag, 1, 0)
    for i in range(6):
        ints[i] = int_out[i]
    for i in range(5):
        flts[i] = flt_out[i]
    ints[COUNTS] = jnp.where(
        lane_col == 0, fill[0], jnp.where(lane_col == 1, fill[1], fill[2])
    )
    flts[DAMP] = jnp.broadcast_to(total(occ_f * rate_b), (rows, width))
    turn = lax.broadcasted_iota(i32, (rows, 1), 0)
    op = own_index + band_size * turn
    here = jnp.where(op < low_count, 1, 0)
    op = jnp.minimum(op, low_count - 1)
    op_mode = total(jnp.where(lane_low == jnp.maximum(op - 1, 0), mark_b, 0.0)) - 1.0
    op_mode = op_mode.astype(i32)
    hit = lane_mode == op_mode
    raised = jnp.where(op >= 1, 1.0, 0.0)
    amp = jnp.sqrt(total(jnp.where(hit, mag_b, 0.0))) * raised
    amp_cos = amp * total(jnp.where(hit, cos_b, 0.0))
    amp_sin = amp * total(jnp.where(hit, sin_b, 0.0))
    damp = total(jnp.where(hit, rate_b, 0.0)) * raised
    ints[OWN_I] = jnp.where(lane_col == 0, here, jnp.where(lane_col == 1, op_mode // EXPS, op))
    flts[OWN_F] = jnp.where(
        lane_col == 0,
        damp,
        jnp.where(lane_col == 1, amp, jnp.where(lane_col == 2, amp_cos, amp_sin)),
    )


def advance_kernel(rho, kprev, out):
    def advance(i, carry):
        for part in range(2):
            out[i, part] = rho[part, i] + section_weight * kprev[part, i]
        return carry

    lax.fori_loop(0, rho.shape[1], advance, 0)


def send_kernel(first_row, blocks, own, asked, y_band, *rest):
    *outs, held, sems, load_sem = rest
    rows = pl.ds(first_row, held.shape[2])
    load = pltpu.make_async_copy(y_band.at[:, :, rows], held, load_sem.at[0])
    load.start()
    load.wait()

    def copies(i, act):
        out_at = 0
        for at, (start, height, steps, inner) in enumerate(blocks):
            place = own[0] // inner
            many = len(outs[out_at].shape) == 4
            for step in range(steps):
                out = outs[out_at + step] if many else outs[out_at].at[:, step]

                def one(p, carry):
                    entry = asked[(place ^ step) * inner + p, 0, 0] if i == 0 else 0
                    act(
                        pltpu.make_async_copy(
                            held.at[entry, :, pl.ds(start, height)],
                            out.at[p],
                            sems.at[at, step * inner + p],
                        )
                    )
                    return carry

                lax.fori_loop(0, inner, one, 0)
            out_at += steps if many else 1

    copies(0, lambda copy: copy.start())
    copies(1, lambda copy: copy.wait())


def low_kernel(
    mine, ints, flts, y_band, rho_own, kprev_own, rho_top, kprev_top, ham, row, keep, give, out, diff, sems
):
    size = out.shape[-1]
    step = pl.program_id(0)
    half = size // 2

    @pl.when(step == 0)
    def _():
        fill_masks(row, diff)

        def clear(j, carry):
            out[0, j] = jnp.zeros((size, size), jnp.float32)
            out[1, j] = jnp.zeros((size, size), jnp.float32)
            return carry

        lax.fori_loop(0, out.shape[1], clear, 0)

        def operator(n, carry):
            def term(c, inner):
                j, s, amp = ints[LOW_J, n, c], ints[LOW_S, n, c], flts[LOW_A, n, c]
                for part in range(2):
                    rows = pl.ds(part * half, half)
                    weight = amp * diff[s, rows]
                    out[0, j, rows] += weight * y_band[n, 1, rows]
                    out[1, j, rows] -= weight * y_band[n, 0, rows]
                return inner

            return lax.fori_loop(0, ints[COUNTS, n, 0], term, carry)

        lax.fori_loop(0, y_band.shape[0], operator, 0)

    @pl.when(ints[OWN_I, step, 0] == 1)
    def _():
        s, j = ints[OWN_I, step, 1], ints[OWN_I, step, 2]
        damping, amp, amp_cos, amp_sin = (flts[OWN_F, step, i] for i in range(4))
        own = rho_own[:, 0] + section_weight * kprev_own[:, 0]
        real, imag = commutator(split(ham[0]), split(ham[1]), own)
        top = rho_top[:, 0] + section_weight * kprev_top[:, 0]
        site_b = jnp.broadcast_to(row[...].astype(jnp.float32), (size, size))
        s_f = lax.convert_element_type(s, jnp.float32)
        va = jnp.where(jnp.transpose(site_b) == s_f, 1.0, 0.0)
        vb = jnp.where(site_b == s_f, 1.0, 0.0)
        w_re, w_im = amp_cos * (va - vb), amp_sin * (va + vb)
        out[0, j] += imag - damping * own[0] + (w_re * top[1] + w_im * top[0])
        out[1, j] += -real - damping * own[1] + (w_im * top[1] - w_re * top[0])
        up = amp * (va - vb)
        out[0, 0] += up * own[1]
        out[1, 0] -= up * own[0]

    @pl.when(step == pl.num_programs(0) - 1)
    def _():
        count = keep.shape[1]
        copies = [
            pltpu.make_async_copy(out.at[:, pl.ds(place * count, count)], to, sems.at[i])
            for i, (place, to) in enumerate(((mine[0], keep), (1 - mine[0], give)))
        ]
        for copy in copies:
            copy.start()
        for copy in copies:
            copy.wait()


def add_terms(n, width, rows, which, ints, flts, fetch, diff, summ, start):
    count_at, source_at, alpha_at = which
    together = math.gcd(width, 8)
    at = n * width

    def terms(g, state):
        re, im = state
        for u in range(together):
            c = at + g * together + u
            m, s = ints[source_at, c], ints[source_at + 1, c]
            w_re = flts[alpha_at, c] * diff[s, rows]
            w_im = flts[alpha_at + 1, c] * summ[s, rows]
            y_re, y_im = fetch(m, rows)
            re = re + (w_re * y_im + w_im * y_re)
            im = im + (w_im * y_im - w_re * y_re)
        return re, im

    groups = (ints[COUNTS, at + count_at] + (together - 1)) // together
    return lax.fori_loop(0, groups, terms, start)


def own_kernel(flts, y_band, ham, out):
    h_re, h_im = split(ham[0]), split(ham[1])

    def operator(n, carry):
        y_pair = y_band[n]
        damping = flts[DAMP, n, 0]
        real, imag = commutator(h_re, h_im, y_pair)
        out[0, n] = imag - damping * y_pair[0]
        out[1, n] = -real - damping * y_pair[1]
        return carry

    lax.fori_loop(0, y_band.shape[0], operator, 0)


def near_kernel(ints, flts, y_band, rho_low, kprev_low, base, row, out, pool, diff, summ):
    size = out.shape[-1]
    low_count, band_count = rho_low.shape[1], y_band.shape[0]
    parts = 2
    fill_masks(row, diff, summ)

    def advance(i, carry):
        for part in range(2):
            pool[i, part] = rho_low[part, i] + section_weight * kprev_low[part, i]
        return carry

    lax.fori_loop(0, low_count, advance, 0)

    def keep(i, carry):
        pool[low_count + i] = y_band[i]
        return carry

    lax.fori_loop(0, band_count, keep, 0)

    def operator(n, carry):
        for part in range(parts):
            rows = pl.ds(part * (size // parts), size // parts)
            re, im = add_terms(
                n,
                ints.shape[1] // band_count,
                rows,
                (1, NEAR_M, NEAR_A),
                ints,
                flts,
                lambda m, r: (pool[m, 0, r], pool[m, 1, r]),
                diff,
                summ,
                (base[0, n, rows], base[1, n, rows]),
            )
            out[0, n, rows] = re
            out[1, n, rows] = im
        return carry

    lax.fori_loop(0, band_count, operator, 0)


def far_kernel(start, ints, flts, base, row, *rest):
    *parts, out, held, received, diff, summ, sems = rest
    block = held.shape[2]
    here = pl.ds(start, block)
    loads = [pltpu.make_async_copy(base.at[:, :, here], held, sems.at[0])]
    if len(parts) == 1:
        loads.append(pltpu.make_async_copy(parts[0], received, sems.at[1]))
    else:
        for step, part in enumerate(parts):
            source = part if step else part.at[:, 0]
            loads.append(pltpu.make_async_copy(source, received.at[:, step], sems.at[1 + step]))
    for load in loads:
        load.start()
    fill_masks(row, diff, summ, start)
    for load in loads:
        load.wait()
    rows = pl.ds(0, block)
    last = received.shape[1] - 1
    shift = last.bit_length()

    def operator(n, carry):
        re, im = add_terms(
            n,
            ints.shape[1] // held.shape[1],
            rows,
            (2, FAR_M, FAR_A),
            ints,
            flts,
            lambda m, r: (received[m >> shift, m & last, 0], received[m >> shift, m & last, 1]),
            diff,
            summ,
            (held[0, n], held[1, n]),
        )
        held[0, n] = re
        held[1, n] = im
        return carry

    lax.fori_loop(0, held.shape[1], operator, 0)
    store = pltpu.make_async_copy(held, out.at[:, :, here], sems.at[0])
    store.start()
    store.wait()


def part_of(x, index, parts, axis):
    step = x.shape[axis] // parts
    return lax.dynamic_slice_in_dim(x, index * step, step, axis)


def join(pieces, indices, axis):
    if len(pieces) == 2:
        first, second = pieces
        return jnp.where(
            indices[0] == 0,
            jnp.concatenate([first, second], axis=axis),
            jnp.concatenate([second, first], axis=axis),
        )
    shape = list(pieces[0].shape)
    step = shape[axis]
    shape[axis] *= len(pieces)
    out = jnp.zeros(shape, pieces[0].dtype)
    for piece, index in zip(pieces, indices):
        out = lax.dynamic_update_slice_in_dim(out, piece, index * step, axis)
    return out


def lay_kernel(places, *refs):
    *pieces, out, sems = refs
    count = pieces[0].shape[0]
    copies = []
    for i, piece in enumerate(pieces):
        core, axis, stream = i // 4, (i // 2) % 2, i % 2
        half = places[0] if core == 0 else 1 - places[0]
        quarter = places[1 + stream] if axis == 0 else 1 - places[1 + stream]
        start = pl.multiple_of((2 * half + quarter) * count, count)
        copies.append(
            pltpu.make_async_copy(piece, out.at[stream, pl.ds(start, count)], sems.at[i])
        )
    for copy in copies:
        copy.start()
    for copy in copies:
        copy.wait()


def sum_over_band(keep, give, band_size, outer, own_index):
    inner = band_size // outer
    bits = inner.bit_length() - 1
    place = own_index // inner
    flag = [(own_index >> b) & 1 for b in range(bits)]
    plain = list(range(1, bits))
    orders = (plain, plain[:2][::-1] + plain[2:])

    def swap(value, distance):
        pairs = [(i, i ^ distance) for i in range(band_size)]
        return lax.ppermute(value, "band", pairs)

    x = keep + swap(give, 1)
    streams = [x[0], x[1]]
    for level in range(bits - 1):
        use = [order[level] for order in orders]
        got = [swap(part_of(v, 1 - flag[b], 2, 0), 1 << b) for v, b in zip(streams, use)]
        streams = [part_of(v, flag[b], 2, 0) + g for v, b, g in zip(streams, use, got)]
    x = jnp.stack(streams)
    got = [swap(part_of(x, place ^ d, outer, 1), d * inner) for d in range(1, outer)]
    x = part_of(x, place, outer, 1)
    for other in got:
        x = x + other
    got = [swap(x, d * inner) for d in range(1, outer)]
    x = join([x] + got, [place ^ d for d in range(outer)], 1)
    streams = [x[0], x[1]]
    for level in reversed(range(1, bits - 1)):
        use = [order[level] for order in orders]
        got = [swap(v, 1 << b) for v, b in zip(streams, use)]
        streams = [
            join([v, g], [flag[b], 1 - flag[b]], 0) for v, b, g in zip(streams, use, got)
        ]
    use = [order[0] for order in orders]
    got = [swap(v, 1 << b) for v, b in zip(streams, use)]
    pieces = streams + got
    pieces += [swap(piece, 1) for piece in pieces]
    places = jnp.stack([flag[0]] + [flag[b] for b in use]).astype(jnp.int32)
    count, width = pieces[0].shape
    return pl.pallas_call(
        lay_kernel,
        in_specs=[smem] + [vmem] * 8,
        out_specs=hbm,
        out_shape=jax.ShapeDtypeStruct((2, 4 * count, width), jnp.float32),
        scratch_shapes=[pltpu.SemaphoreType.DMA((8,))],
        compiler_params=pltpu.CompilerParams(vmem_limit_bytes=VMEM_LIMIT),
        name="lay",
    )(places, *pieces)


def shards(
    rho_low,
    kprev_low,
    rho_band,
    kprev_band,
    hamiltonian,
    state_site,
    coupling_mag,
    coupling_phase,
    damping_rate,
    low_mode,
    occupation,
    couple_src,
    couple_mode,
    couple_dir,
):
    band_size = lax.axis_size("band")
    own_index = lax.axis_index("band")
    low_count = rho_low.shape[1]
    band_count = rho_band.shape[1]
    size = rho_band.shape[-1]
    sites = coupling_mag.shape[0] // EXPS
    f32 = jnp.float32
    params = functools.partial(pltpu.CompilerParams, vmem_limit_bytes=VMEM_LIMIT)

    shifted = couple_src - low_count
    owner = jnp.where(couple_src >= low_count, shifted // band_count, own_index)
    slot = jnp.where(owner != own_index, shifted % band_count, 0)
    asks = owner[None] == jnp.arange(band_size)[:, None, None]
    wanted = jnp.max(jnp.where(asks, slot[None], 0), axis=(1, 2))
    wanted = jnp.broadcast_to(wanted[:, None, None], (band_size, 1, 128))
    asked = lax.all_to_all(wanted, "band", split_axis=0, concat_axis=0, tiled=True)

    outer = OUTER if band_size % OUTER == 0 else 1
    inner = band_size // outer
    own = jnp.stack([own_index, jnp.int32(band_size), jnp.int32(inner)]).astype(jnp.int32)
    heights = [size * part // sum(BLOCKS) for part in BLOCKS]
    starts = [sum(heights[:i]) for i in range(len(heights))]
    y_band = pl.pallas_call(
        advance_kernel,
        in_specs=[vmem, vmem],
        out_specs=vmem,
        out_shape=jax.ShapeDtypeStruct((band_count, 2, size, size), f32),
        compiler_params=params(),
        name="advance",
    )(rho_band, kprev_band)
    last = len(starts) - 1
    send = []
    for which in (slice(0, 1), slice(1, None)):
        first_row, last_row = starts[which][0], starts[which][-1] + heights[which][-1]
        shapes = []
        for height in heights[which][: None if which.start == 0 else -1]:
            shapes += [(inner, 2, height, size)] * outer
        if which.start:
            shapes.append((inner, outer, 2, heights[last], size))
        send += pl.pallas_call(
            functools.partial(
                send_kernel,
                first_row,
                [(s - first_row, h, outer, inner) for s, h in zip(starts[which], heights[which])],
            ),
            in_specs=[smem, smem, hbm],
            out_specs=[hbm] * len(shapes),
            out_shape=[jax.ShapeDtypeStruct(shape, f32) for shape in shapes],
            scratch_shapes=[
                pltpu.VMEM((band_count, 2, last_row - first_row, size), f32),
                pltpu.SemaphoreType.DMA((len(starts[which]), band_size)),
                pltpu.SemaphoreType.DMA((1,)),
            ],
            compiler_params=params(),
        )(own, asked, y_band)

    groups = [[o * inner + p for p in range(inner)] for o in range(outer)]

    def go_out(value, step):
        pairs = [(i, i ^ (step * inner)) for i in range(band_size)]
        return lax.ppermute(value, "band", pairs)

    def go_in(value):
        return lax.all_to_all(
            value, "band", split_axis=0, concat_axis=0, tiled=True, axis_index_groups=groups
        )

    received = []
    for block in range(last):
        first = send[block * outer : (block + 1) * outer]
        moved = [first[0]] + [go_out(first[step], step) for step in range(1, outer)]
        received.append([go_in(jnp.stack(moved, axis=1))])
    first = go_in(send[-1])
    received.append([first] + [go_out(first[:, step], step) for step in range(1, outer)])

    whole_row = (1, -1)
    ints, flts = pl.pallas_call(
        functools.partial(prep_kernel, low_count),
        in_specs=[smem] + [vmem] * 9,
        out_specs=[vmem, vmem],
        out_shape=[
            jax.ShapeDtypeStruct((8,) + couple_src.shape, jnp.int32),
            jax.ShapeDtypeStruct((7,) + couple_src.shape, f32),
        ],
        name="prep",
    )(
        own,
        couple_src,
        couple_mode,
        couple_dir,
        occupation,
        coupling_mag.reshape(whole_row),
        jnp.cos(coupling_phase).reshape(whole_row),
        jnp.sin(coupling_phase).reshape(whole_row),
        damping_rate.reshape(whole_row),
        low_mode.reshape(whole_row),
    )

    row = state_site[None, :]

    ints_flat, flts_flat = ints.reshape(8, -1), flts.reshape(7, -1)

    turns = -(-low_count // band_size)
    own_op = jnp.minimum(
        own_index + band_size * jnp.arange(turns, dtype=jnp.int32), low_count - 1
    )
    own_block = pl.BlockSpec((2, 1, size, size), lambda g, ops: (0, ops[g], 0, 0))
    top_block = pl.BlockSpec((2, 1, size, size), lambda g, ops: (0, 0, 0, 0))
    half_shape = (2, low_count // 2, size, size)
    keep, give = pl.pallas_call(
        lambda ops, *refs: low_kernel(*refs),
        grid_spec=pltpu.PrefetchScalarGridSpec(
            num_scalar_prefetch=1,
            grid=(turns,),
            in_specs=[smem] * 3
            + [vmem, own_block, own_block, top_block, top_block]
            + [vmem] * 2,
            out_specs=[hbm] * 2,
            scratch_shapes=[
                pltpu.VMEM((2, low_count, size, size), f32),
                pltpu.VMEM((sites, size, size), f32),
                pltpu.SemaphoreType.DMA((2,)),
            ],
        ),
        out_shape=[jax.ShapeDtypeStruct(half_shape, f32)] * 2,
        compiler_params=params(),
        name="low",
    )(
        own_op,
        (own_index & 1).astype(jnp.int32)[None],
        ints,
        flts,
        y_band,
        rho_low,
        kprev_low,
        rho_low,
        kprev_low,
        hamiltonian,
        row,
    )
    flat = (2, -1, size)
    k_low = sum_over_band(keep.reshape(flat), give.reshape(flat), band_size, outer, own_index)
    k_low = k_low.reshape(rho_low.shape)

    base = pl.pallas_call(
        own_kernel,
        in_specs=[smem] + [vmem] * 2,
        out_specs=vmem,
        out_shape=jax.ShapeDtypeStruct((2, band_count, size, size), f32),
        compiler_params=params(),
        name="own",
    )(flts, y_band, hamiltonian)

    def far_terms(k_band, block):
        height = heights[block]
        parts = received[block]
        return pl.pallas_call(
            functools.partial(far_kernel, starts[block]),
            in_specs=[smem] * 2 + [hbm, vmem] + [hbm] * len(parts),
            out_specs=hbm,
            out_shape=jax.ShapeDtypeStruct((2, band_count, size, size), f32),
            scratch_shapes=[pltpu.VMEM((2, band_count, height, size), f32)]
            + [pltpu.VMEM((inner, outer, 2, height, size), f32)]
            + [pltpu.VMEM((sites, height, size), f32)] * 2
            + [pltpu.SemaphoreType.DMA((1 + len(parts),))],
            input_output_aliases={2: 0},
            compiler_params=params(),
        )(ints_flat, flts_flat, k_band, row, *parts)

    k_band = base
    for block in range(last):
        k_band = far_terms(k_band, block)
    k_band = pl.pallas_call(
        near_kernel,
        in_specs=[smem] * 2 + [vmem] * 5,
        out_specs=vmem,
        out_shape=jax.ShapeDtypeStruct((2, band_count, size, size), f32),
        scratch_shapes=[pltpu.VMEM((low_count + band_count, 2, size, size), f32)]
        + [pltpu.VMEM((sites, size, size), f32)] * 2,
        compiler_params=params(),
        name="near",
    )(ints_flat, flts_flat, y_band, rho_low, kprev_low, k_band, row)
    k_band = far_terms(k_band, last)
    return (k_low, k_band)


def solution(mesh):
    placed = (
        P(),
        P(),
        P(None, "band", None, None),
        P(None, "band", None, None),
        P(),
        P(),
        P(),
        P(),
        P(),
        P(),
        P("band", None),
        P("band", None),
        P("band", None),
        P("band", None),
    )
    return jax.shard_map(
        shards,
        mesh=mesh,
        in_specs=placed,
        out_specs=(P(), P(None, "band", None, None)),
        check_vma=False,
    )
```

profile of v0, /device:TPU:0, one launch (start us, length us, event | category | flops | bytes accessed | tf_op | source)
XLA Modules:
  0.0 251.3 jit_solution(1195238886109454782)
XLA Ops:
  2.4 3.8 %advance.1.refs_3_.y_band = f32[16,2,128,128]{3,2,1,0:T(8,128)} custom-call(f32[2,16,128,128]{3,2,1,0:T(8,128)} %rho.1, f32[2,16,128,128]{3,2,1,0:T(8,128)} %kprev.1), custom_call_target="tpu_custom_call" | custom-call | tf_op jit(solution)/shard_map/advance/pallas_call | solution.py:513
  6.3 6.2 %prep.1 = (s32[8,16,16]{2,1,0:T(8,128)}, f32[7,16,16]{2,1,0:T(8,128)}) custom-call(s32[3]{0:T(128)} %pad_add_fusion.1.own, s32[16,16]{1,0:T(8,128)} %src.1, s32[16,16]{1,0:T(8,128)} %mode.1, s32[16,16]{1,0:T(8,128)} %direction.1, s32[16,72]{1,0:T(8,128)} %occ.1, f32[1,72]{1,0:T(1,128)} %bitcast.65, f32[1,72]{1,0:T(1,128)} %get-tuple-element.43.cos, ...), custom_call_target="tpu_custom_call" | custom-call | tf_op jit(solution)/shard_map/prep/pallas_call | solution.py:567
  12.5 7.4 %low.1 = (f32[2,16,128,128]{3,2,1,0:T(8,128)}, f32[2,16,128,128]{3,2,1,0:T(8,128)}) custom-call(s32[1]{0:T(128)S(6)} %min.3.ops, s32[1]{0:T(128)} %bitcast.4.refs_0_, s32[8,16,16]{2,1,0:T(8,128)} %get-tuple-element.15.refs_1_, f32[7,16,16]{2,1,0:T(8,128)} %get-tuple-element.16.refs_2_.flts, f32[16,2,128,128]{3,2,1,0:T(8,128)} %advance.1.refs_3_.y_band, ...), custom_call_target="tpu_custom_call" | custom-call | tf_op jit(solution)/shard_map/low/pallas_call | solution.py:600
  20.4 4.0 %collective-permute-done = f32[2,2048,128]{2,1,0:T(8,128)S(1)} collective-permute-done((f32[2,2048,128]{2,1,0:T(8,128)}, f32[2,2048,128]{2,1,0:T(8,128)S(1)}, u32[]{:S(2)}, u32[]{:S(2)}) %collective-permute-start) | collective-permute-done | bytes 2097184 | tf_op jit(solution)/shard_map/ppermute | solution.py:436
  27.1 3.1 %collective-permute-start.1 = (f32[1024,128]{1,0:T(8,128)}, f32[1024,128]{1,0:T(8,128)}, u32[]{:S(2)}, u32[]{:S(2)}) collective-permute-start(f32[1024,128]{1,0:T(8,128)} %dynamic-slice_bitcast_fusion.1), channel_id=1, source_target_pairs={{0,2},{1,3},{2,0},{3,1},{4,6},{5,7},{6,4},{7,5},{8,10},{9,11},{10,... | collective-permute-start | bytes 1572872 | tf_op jit(solution)/shard_map/ppermute | solution.py:436
  30.5 13.6 %all_to_all.20.asked = s32[32,1,128]{2,1,0:T(1,128)} all-to-all(s32[32,1,128]{2,1,0:T(1,128)S(1)} %broadcast_in_dim.42), channel_id=1, replica_groups=mesh['band'=32] {'band'}, dimensions={0} | all-to-all | bytes 32768 | tf_op jit(solution)/shard_map/all_to_all | solution.py:506
  44.1 3.2 %shard_map.149 = (f32[8,2,32,128]{3,2,1,0:T(8,128)}, f32[8,2,32,128]{3,2,1,0:T(8,128)}, f32[8,2,32,128]{3,2,1,0:T(8,128)}, f32[8,2,32,128]{3,2,1,0:T(8,128)}) custom-call(s32[3]{0:T(128)} %pad_add_fusion.1.own, s32[32,1,128]{2,1,0:T(1,128)} %all_to_all.20.asked, f32[16,2,128,128]{3,2,1,0:T(8,128)} %advance.1.refs_3_.y_band), custom_call_target="tpu_custom_call" | custom-call | tf_op jit(solution)/shard_map/pallas_call | solution.py:530
  53.3 7.3 %collective-permute-done.19 = f32[8,2,32,128]{3,2,1,0:T(8,128)S(1)} collective-permute-done((f32[8,2,32,128]{3,2,1,0:T(8,128)}, f32[8,2,32,128]{3,2,1,0:T(8,128)S(1)}, u32[]{:S(2)}, u32[]{:S(2)}) %collective-permute-start.19) | collective-permute-done | bytes 262176 | tf_op jit(solution)/shard_map/ppermute | solution.py:551
  60.6 9.4 %collective-permute-done.20 = f32[8,2,32,128]{3,2,1,0:T(8,128)S(1)} collective-permute-done((f32[8,2,32,128]{3,2,1,0:T(8,128)}, f32[8,2,32,128]{3,2,1,0:T(8,128)S(1)}, u32[]{:S(2)}, u32[]{:S(2)}) %collective-permute-start.20) | collective-permute-done | bytes 262176 | tf_op jit(solution)/shard_map/ppermute | solution.py:551
  72.0 3.6 %all-to-all-start.1 = ((f32[8,4,2,32,128]{4,3,2,1,0:T(8,128)}), f32[8,4,2,32,128]{4,3,2,1,0:T(8,128)S(1)}, u32[]{:S(2)}, u32[]{:S(2)}) async-start(f32[8,4,2,32,128]{4,3,2,1,0:T(8,128)} %pad_maximum_fusion.1), calls=%async_computation.1 | async-start | bytes 2097152 | tf_op jit(solution)/shard_map/all_to_all | solution.py:554
  81.4 14.1 %collective-permute-done.2 = f32[512,128]{1,0:T(8,128)S(1)} collective-permute-done((f32[512,128]{1,0:T(8,128)S(1)}, f32[512,128]{1,0:T(8,128)S(1)}, u32[]{:S(2)}, u32[]{:S(2)}) %collective-permute-start.2) | collective-permute-done | bytes 262176 | tf_op jit(solution)/shard_map/ppermute | solution.py:436
  96.6 5.0 %collective-permute-start.5 = (f32[2,128,128]{2,1,0:T(8,128)S(1)}, f32[2,128,128]{2,1,0:T(8,128)S(1)}, u32[]{:S(2)}, u32[]{:S(2)}) collective-permute-start(f32[2,128,128]{2,1,0:T(8,128)S(1)} %get-tuple-element.37), channel_id=1, source_target_pairs={{0,8},{1,9},{2,10},{3,11},{4,12},{5,13},{6,14},{7,15},{8,0},{9,1},... | collective-permute-start | bytes 393224 | tf_op jit(solution)/shard_map/ppermute | solution.py:436
  104.4 4.5 %shard_map.151 = (f32[8,2,40,128]{3,2,1,0:T(8,128)}, f32[8,2,40,128]{3,2,1,0:T(8,128)}, f32[8,2,40,128]{3,2,1,0:T(8,128)}, f32[8,2,40,128]{3,2,1,0:T(8,128)}, f32[8,4,2,56,128]{4,3,2,1,0:T(8,128)}) custom-call(s32[3]{0:T(128)} %pad_add_fusion.1.own, s32[32,1,128]{2,1,0:T(1,128)} %all_to_all.20.asked, f32[16,2,128,128]{3,2,1,0:T(8,128)} %advance.1.refs_3_.y_band), custom_call_target="tpu_custom_call" | custom-call | tf_op jit(solution)/shard_map/pallas_call | solution.py:530
  109.9 3.6 %all-to-all-start.3 = ((f32[8,4,2,56,128]{4,3,2,1,0:T(8,128)}), f32[8,4,2,56,128]{4,3,2,1,0:T(8,128)S(1)}, u32[]{:S(2)}, u32[]{:S(2)}) async-start(f32[8,4,2,56,128]{4,3,2,1,0:T(8,128)} %get-tuple-element.27), calls=%async_computation.3 | async-start | bytes 3670016 | tf_op jit(solution)/shard_map/all_to_all | solution.py:554
  126.5 23.0 %collective-permute-done.10 = f32[2,128,128]{2,1,0:T(8,128)S(1)} collective-permute-done((f32[2,128,128]{2,1,0:T(8,128)S(1)}, f32[2,128,128]{2,1,0:T(8,128)S(1)}, u32[]{:S(2)}, u32[]{:S(2)}) %collective-permute-start.10) | collective-permute-done | bytes 131104 | tf_op jit(solution)/shard_map/ppermute | solution.py:436
  160.5 3.6 %all-to-all-start.2 = ((f32[8,4,2,40,128]{4,3,2,1,0:T(8,128)}), f32[8,4,2,40,128]{4,3,2,1,0:T(8,128)S(1)}, u32[]{:S(2)}, u32[]{:S(2)}) async-start(f32[8,4,2,40,128]{4,3,2,1,0:T(8,128)} %pad_maximum_fusion), calls=%async_computation.2 | async-start | bytes 2621440 | tf_op jit(solution)/shard_map/all_to_all | solution.py:554
  166.7 10.9 %collective-permute-start.26 = (f32[8,2,56,128]{3,2,1,0:T(8,128)S(1)}, f32[8,2,56,128]{3,2,1,0:T(8,128)}, u32[]{:S(2)}, u32[]{:S(2)}) collective-permute-start(f32[8,2,56,128]{3,2,1,0:T(8,128)S(1)} %get-tuple-element.33), channel_id=1, source_target_pairs={{0,16},{1,17},{2,18},{3,19},{4,20},{5,21},{6,22},{7,23},{8,24},{9,... | collective-permute-start | bytes 1376264 | tf_op jit(solution)/shard_map/ppermute | solution.py:551
  180.4 28.8 %collective-permute-done.26.rest_2_ = f32[8,2,56,128]{3,2,1,0:T(8,128)} collective-permute-done((f32[8,2,56,128]{3,2,1,0:T(8,128)S(1)}, f32[8,2,56,128]{3,2,1,0:T(8,128)}, u32[]{:S(2)}, u32[]{:S(2)}) %collective-permute-start.26) | collective-permute-done | bytes 458784 | tf_op jit(solution)/shard_map/ppermute | solution.py:551
  210.6 8.0 %own.1.base = f32[2,16,128,128]{3,2,1,0:T(8,128)} custom-call(f32[7,16,16]{2,1,0:T(8,128)} %get-tuple-element.16.refs_2_.flts, f32[16,2,128,128]{3,2,1,0:T(8,128)} %advance.1.refs_3_.y_band, f32[2,128,128]{2,1,0:T(8,128)} %ham.1), custom_call_target="tpu_custom_call" | custom-call | tf_op jit(solution)/shard_map/own/pallas_call | solution.py:635
  219.3 4.4 %shard_map.150.base = f32[2,16,128,128]{3,2,1,0:T(8,128)} custom-call(s32[8,256]{1,0:T(8,128)} %reshape.51.ints, f32[7,256]{1,0:T(8,128)} %reshape.52.flts, f32[2,16,128,128]{3,2,1,0:T(8,128)} %own.1.base, s32[1,128]{1,0:T(1,128)} %bitcast.61, f32[8,4,2,32,128]{4,3,2,1,0:T(8,128)} %copy-done.2), custom_call_target="tpu_custom_call", output_to_operand_aliasing={{}: (2, {})} | custom-call | tf_op jit(solution)/shard_map/pallas_call | solution.py:647
  224.8 4.7 %shard_map.152.base = f32[2,16,128,128]{3,2,1,0:T(8,128)} custom-call(s32[8,256]{1,0:T(8,128)} %reshape.51.ints, f32[7,256]{1,0:T(8,128)} %reshape.52.flts, f32[2,16,128,128]{3,2,1,0:T(8,128)} %shard_map.150.base, s32[1,128]{1,0:T(1,128)} %bitcast.62, f32[8,4,2,40,128]{4,3,2,1,0:T(8,128)} %copy-done.1), custom_call_target="tpu_custom_call", output_to_operand_aliasing={{}: (2, {})} | custom-call | tf_op jit(solution)/shard_map/pallas_call | solution.py:647
  229.5 11.1 %near.1.base = f32[2,16,128,128]{3,2,1,0:T(8,128)} custom-call(s32[8,256]{1,0:T(8,128)} %reshape.51.ints, f32[7,256]{1,0:T(8,128)} %reshape.52.flts, f32[16,2,128,128]{3,2,1,0:T(8,128)} %advance.1.refs_3_.y_band, f32[2,32,128,128]{3,2,1,0:T(8,128)} %rho_low.1, f32[2,32,128,128]{3,2,1,0:T(8,128)} %kprev_low.1, f32[2,16,128,128]{3,2,1,0:T(8,128)} %shard_map.152.base, ...), custom_call_target="tpu_custom_call" | custom-call | tf_op jit(solution)/shard_map/near/pallas_call | solution.py:663
  240.6 5.4 %shard_map.153 = f32[2,16,128,128]{3,2,1,0:T(8,128)} custom-call(s32[8,256]{1,0:T(8,128)} %reshape.51.ints, f32[7,256]{1,0:T(8,128)} %reshape.52.flts, f32[2,16,128,128]{3,2,1,0:T(8,128)} %near.1.base, s32[1,128]{1,0:T(1,128)} %bitcast.64, f32[8,4,2,56,128]{4,3,2,1,0:T(8,128)} %copy-done, ...), custom_call_target="tpu_custom_call", output_to_operand_aliasing={{}: (2, {})} | custom-call | tf_op jit(solution)/shard_map/pallas_call | solution.py:647
  247.1 4.2 %lay.1 = f32[2,4096,128]{2,1,0:T(8,128)} custom-call(s32[3]{0:T(128)} %pad_add_fusion.places, f32[1024,128]{1,0:T(8,128)} %maximum_select_fusion.refs_0_, f32[1024,128]{1,0:T(8,128)} %maximum_select_fusion.1.refs_1_, f32[1024,128]{1,0:T(8,128)} %collective-permute-done.13.refs_2_, f32[1024,128]{1,0:T(8,128)} %collective-permute-done.14.refs_3_, ...), custom_call_target="tpu_custom_call" | custom-call | tf_op jit(solution)/shard_map/lay/pallas_call | solution.py:464
  (102 shorter events, 57.4 us)
Async XLA Ops:
  27.1 48.5 %collective-permute-start.1 = (f32[1024,128]{1,0:T(8,128)}, f32[1024,128]{1,0:T(8,128)}, u32[]{:S(2)}, u32[]{:S(2)}) collective-permute-start(f32[1024,128]{1,0:T(8,128)} %dynamic-slice_bitcast_fusion.1), channel_id=1, source_target_pairs={{0,2},{1,3},{2,0},{3,1},{4,6},{5,7},{6,4},{7,5},{8,10},{9,11},{10,... | collective-permute-start | bytes 1572872 | tf_op jit(solution)/shard_map/ppermute | solution.py:436
  47.4 13.2 %collective-permute-start.19 = (f32[8,2,32,128]{3,2,1,0:T(8,128)}, f32[8,2,32,128]{3,2,1,0:T(8,128)S(1)}, u32[]{:S(2)}, u32[]{:S(2)}) collective-permute-start(f32[8,2,32,128]{3,2,1,0:T(8,128)} %get-tuple-element.20), channel_id=1, source_target_pairs={{0,8},{1,9},{2,10},{3,11},{4,12},{5,13},{6,14},{7,15},{8,0},{9,1},... | collective-permute-start | bytes 786440 | tf_op jit(solution)/shard_map/ppermute | solution.py:551
  48.5 21.5 %collective-permute-start.20 = (f32[8,2,32,128]{3,2,1,0:T(8,128)}, f32[8,2,32,128]{3,2,1,0:T(8,128)S(1)}, u32[]{:S(2)}, u32[]{:S(2)}) collective-permute-start(f32[8,2,32,128]{3,2,1,0:T(8,128)} %get-tuple-element.21), channel_id=1, source_target_pairs={{0,16},{1,17},{2,18},{3,19},{4,20},{5,21},{6,22},{7,23},{8,24},{9,... | collective-permute-start | bytes 786440 | tf_op jit(solution)/shard_map/ppermute | solution.py:551
  51.3 18.7 %collective-permute-start.21 = (f32[8,2,32,128]{3,2,1,0:T(8,128)}, f32[8,2,32,128]{3,2,1,0:T(8,128)S(1)}, u32[]{:S(2)}, u32[]{:S(2)}) collective-permute-start(f32[8,2,32,128]{3,2,1,0:T(8,128)} %get-tuple-element.22), channel_id=1, source_target_pairs={{0,24},{1,25},{2,26},{3,27},{4,28},{5,29},{6,30},{7,31},{8,16},{9,... | collective-permute-start | bytes 786440 | tf_op jit(solution)/shard_map/ppermute | solution.py:551
  52.6 26.1 %collective-permute-start.3 = (f32[1024,128]{1,0:T(8,128)}, f32[1024,128]{1,0:T(8,128)}, u32[]{:S(2)}, u32[]{:S(2)}) collective-permute-start(f32[1024,128]{1,0:T(8,128)} %dynamic-slice_bitcast_fusion), channel_id=1, source_target_pairs={{0,4},{1,5},{2,6},{3,7},{4,0},{5,1},{6,2},{7,3},{8,12},{9,13},{10,... | collective-permute-start | bytes 1572872 | tf_op jit(solution)/shard_map/ppermute | solution.py:436
  72.0 36.9 %all-to-all-start.1 = ((f32[8,4,2,32,128]{4,3,2,1,0:T(8,128)}), f32[8,4,2,32,128]{4,3,2,1,0:T(8,128)S(1)}, u32[]{:S(2)}, u32[]{:S(2)}) async-start(f32[8,4,2,32,128]{4,3,2,1,0:T(8,128)} %pad_maximum_fusion.1), calls=%async_computation.1 | async-start | bytes 2097152 | tf_op jit(solution)/shard_map/all_to_all | solution.py:554
  76.7 18.8 %collective-permute-start.2 = (f32[512,128]{1,0:T(8,128)S(1)}, f32[512,128]{1,0:T(8,128)S(1)}, u32[]{:S(2)}, u32[]{:S(2)}) collective-permute-start(f32[512,128]{1,0:T(8,128)S(1)} %constant_dynamic-slice_fusion.1), channel_id=1, source_target_pairs={{0,4},{1,5},{2,6},{3,7},{4,0},{5,1},{6,2},{7,3},{8,12},{9,13},{10,... | collective-permute-start | bytes 786440 | tf_op jit(solution)/shard_map/ppermute | solution.py:436
  79.9 16.7 %collective-permute-start.4 = (f32[512,128]{1,0:T(8,128)S(1)}, f32[512,128]{1,0:T(8,128)S(1)}, u32[]{:S(2)}, u32[]{:S(2)}) collective-permute-start(f32[512,128]{1,0:T(8,128)S(1)} %constant_dynamic-slice_fusion), channel_id=1, source_target_pairs={{0,2},{1,3},{2,0},{3,1},{4,6},{5,7},{6,4},{7,5},{8,10},{9,11},{10,... | collective-permute-start | bytes 786440 | tf_op jit(solution)/shard_map/ppermute | solution.py:436
  96.6 16.9 %collective-permute-start.5 = (f32[2,128,128]{2,1,0:T(8,128)S(1)}, f32[2,128,128]{2,1,0:T(8,128)S(1)}, u32[]{:S(2)}, u32[]{:S(2)}) collective-permute-start(f32[2,128,128]{2,1,0:T(8,128)S(1)} %get-tuple-element.37), channel_id=1, source_target_pairs={{0,8},{1,9},{2,10},{3,11},{4,12},{5,13},{6,14},{7,15},{8,0},{9,1},... | collective-permute-start | bytes 393224 | tf_op jit(solution)/shard_map/ppermute | solution.py:436
  109.9 50.6 %all-to-all-start.3 = ((f32[8,4,2,56,128]{4,3,2,1,0:T(8,128)}), f32[8,4,2,56,128]{4,3,2,1,0:T(8,128)S(1)}, u32[]{:S(2)}, u32[]{:S(2)}) async-start(f32[8,4,2,56,128]{4,3,2,1,0:T(8,128)} %get-tuple-element.27), calls=%async_computation.3 | async-start | bytes 3670016 | tf_op jit(solution)/shard_map/all_to_all | solution.py:554
  118.6 33.5 %collective-permute-start.22 = (f32[8,2,40,128]{3,2,1,0:T(8,128)}, f32[8,2,40,128]{3,2,1,0:T(8,128)S(1)}, u32[]{:S(2)}, u32[]{:S(2)}) collective-permute-start(f32[8,2,40,128]{3,2,1,0:T(8,128)} %get-tuple-element.24), channel_id=1, source_target_pairs={{0,8},{1,9},{2,10},{3,11},{4,12},{5,13},{6,14},{7,15},{8,0},{9,1},... | collective-permute-start | bytes 983048 | tf_op jit(solution)/shard_map/ppermute | solution.py:551
  120.6 31.5 %collective-permute-start.23 = (f32[8,2,40,128]{3,2,1,0:T(8,128)}, f32[8,2,40,128]{3,2,1,0:T(8,128)}, u32[]{:S(2)}, u32[]{:S(2)}) collective-permute-start(f32[8,2,40,128]{3,2,1,0:T(8,128)} %get-tuple-element.25), channel_id=1, source_target_pairs={{0,16},{1,17},{2,18},{3,19},{4,20},{5,21},{6,22},{7,23},{8,24},{9,... | collective-permute-start | bytes 983048 | tf_op jit(solution)/shard_map/ppermute | solution.py:551
  120.6 31.5 %collective-permute-start.24 = (f32[8,2,40,128]{3,2,1,0:T(8,128)}, f32[8,2,40,128]{3,2,1,0:T(8,128)}, u32[]{:S(2)}, u32[]{:S(2)}) collective-permute-start(f32[8,2,40,128]{3,2,1,0:T(8,128)} %get-tuple-element.26), channel_id=1, source_target_pairs={{0,24},{1,25},{2,26},{3,27},{4,28},{5,29},{6,30},{7,31},{8,16},{9,... | collective-permute-start | bytes 983048 | tf_op jit(solution)/shard_map/ppermute | solution.py:551
  125.0 24.4 %collective-permute-start.10 = (f32[2,128,128]{2,1,0:T(8,128)S(1)}, f32[2,128,128]{2,1,0:T(8,128)S(1)}, u32[]{:S(2)}, u32[]{:S(2)}) collective-permute-start(f32[2,128,128]{2,1,0:T(8,128)S(1)} %get-tuple-element.29), channel_id=1, source_target_pairs={{0,24},{1,25},{2,26},{3,27},{4,28},{5,29},{6,30},{7,31},{8,16},{9,... | collective-permute-start | bytes 393224 | tf_op jit(solution)/shard_map/ppermute | solution.py:436
  157.1 22.8 %collective-permute-start.13 = (f32[1024,128]{1,0:T(8,128)}, f32[1024,128]{1,0:T(8,128)}, u32[]{:S(2)}, u32[]{:S(2)}) collective-permute-start(f32[1024,128]{1,0:T(8,128)} %maximum_select_fusion.refs_0_), channel_id=1, source_target_pairs={{0,2},{1,3},{2,0},{3,1},{4,6},{5,7},{6,4},{7,5},{8,10},{9,11},{10,... | collective-permute-start | bytes 1572872 | tf_op jit(solution)/shard_map/ppermute | solution.py:436
  160.2 20.2 %collective-permute-start.14 = (f32[1024,128]{1,0:T(8,128)}, f32[1024,128]{1,0:T(8,128)}, u32[]{:S(2)}, u32[]{:S(2)}) collective-permute-start(f32[1024,128]{1,0:T(8,128)} %maximum_select_fusion.1.refs_1_), channel_id=1, source_target_pairs={{0,4},{1,5},{2,6},{3,7},{4,0},{5,1},{6,2},{7,3},{8,12},{9,13},{10,... | collective-permute-start | bytes 1572872 | tf_op jit(solution)/shard_map/ppermute | solution.py:436
  160.5 63.2 %all-to-all-start.2 = ((f32[8,4,2,40,128]{4,3,2,1,0:T(8,128)}), f32[8,4,2,40,128]{4,3,2,1,0:T(8,128)S(1)}, u32[]{:S(2)}, u32[]{:S(2)}) async-start(f32[8,4,2,40,128]{4,3,2,1,0:T(8,128)} %pad_maximum_fusion), calls=%async_computation.2 | async-start | bytes 2621440 | tf_op jit(solution)/shard_map/all_to_all | solution.py:554
  165.0 14.8 %collective-permute-start.27 = (f32[8,2,56,128]{3,2,1,0:T(8,128)S(1)}, f32[8,2,56,128]{3,2,1,0:T(8,128)}, u32[]{:S(2)}, u32[]{:S(2)}) collective-permute-start(f32[8,2,56,128]{3,2,1,0:T(8,128)S(1)} %get-tuple-element.32), channel_id=1, source_target_pairs={{0,24},{1,25},{2,26},{3,27},{4,28},{5,29},{6,30},{7,31},{8,16},{9,... | collective-permute-start | bytes 1376264 | tf_op jit(solution)/shard_map/ppermute | solution.py:551
  166.7 42.6 %collective-permute-start.26 = (f32[8,2,56,128]{3,2,1,0:T(8,128)S(1)}, f32[8,2,56,128]{3,2,1,0:T(8,128)}, u32[]{:S(2)}, u32[]{:S(2)}) collective-permute-start(f32[8,2,56,128]{3,2,1,0:T(8,128)S(1)} %get-tuple-element.33), channel_id=1, source_target_pairs={{0,16},{1,17},{2,18},{3,19},{4,20},{5,21},{6,22},{7,23},{8,24},{9,... | collective-permute-start | bytes 1376264 | tf_op jit(solution)/shard_map/ppermute | solution.py:551
  177.6 68.4 %collective-permute-start.15 = (f32[1024,128]{1,0:T(8,128)}, f32[1024,128]{1,0:T(8,128)S(1)}, u32[]{:S(2)}, u32[]{:S(2)}) collective-permute-start(f32[1024,128]{1,0:T(8,128)} %maximum_select_fusion.refs_0_), channel_id=1, source_target_pairs={{0,1},{1,0},{2,3},{3,2},{4,5},{5,4},{6,7},{7,6},{8,9},{9,8},{10,11... | collective-permute-start | bytes 1572872 | tf_op jit(solution)/shard_map/ppermute | solution.py:436
  179.9 66.1 %collective-permute-start.16 = (f32[1024,128]{1,0:T(8,128)}, f32[1024,128]{1,0:T(8,128)S(1)}, u32[]{:S(2)}, u32[]{:S(2)}) collective-permute-start(f32[1024,128]{1,0:T(8,128)} %maximum_select_fusion.1.refs_1_), channel_id=1, source_target_pairs={{0,1},{1,0},{2,3},{3,2},{4,5},{5,4},{6,7},{7,6},{8,9},{9,8},{10,11... | collective-permute-start | bytes 1572872 | tf_op jit(solution)/shard_map/ppermute | solution.py:436
  179.9 66.1 %collective-permute-start.17 = (f32[1024,128]{1,0:T(8,128)}, f32[1024,128]{1,0:T(8,128)S(1)}, u32[]{:S(2)}, u32[]{:S(2)}) collective-permute-start(f32[1024,128]{1,0:T(8,128)} %collective-permute-done.13.refs_2_), channel_id=1, source_target_pairs={{0,1},{1,0},{2,3},{3,2},{4,5},{5,4},{6,7},{7,6},{8,9},{9,8},{10,11... | collective-permute-start | bytes 1572872 | tf_op jit(solution)/shard_map/ppermute | solution.py:436
  180.4 65.6 %collective-permute-start.18 = (f32[1024,128]{1,0:T(8,128)}, f32[1024,128]{1,0:T(8,128)}, u32[]{:S(2)}, u32[]{:S(2)}) collective-permute-start(f32[1024,128]{1,0:T(8,128)} %collective-permute-done.14.refs_3_), channel_id=1, source_target_pairs={{0,1},{1,0},{2,3},{3,2},{4,5},{5,4},{6,7},{7,6},{8,9},{9,8},{10,11... | collective-permute-start | bytes 1572872 | tf_op jit(solution)/shard_map/ppermute | solution.py:436
  209.3 31.3 %collective-permute-start.25 = (f32[8,2,56,128]{3,2,1,0:T(8,128)}, f32[8,2,56,128]{3,2,1,0:T(8,128)}, u32[]{:S(2)}, u32[]{:S(2)}) collective-permute-start(f32[8,2,56,128]{3,2,1,0:T(8,128)} %get-tuple-element.34), channel_id=1, source_target_pairs={{0,8},{1,9},{2,10},{3,11},{4,12},{5,13},{6,14},{7,15},{8,0},{9,1},... | collective-permute-start | bytes 1376264 | tf_op jit(solution)/shard_map/ppermute | solution.py:551
  (18 other events, 220.5 us)
where the time goes:
time: 253 us; the launch traced here: 251 us
  waiting for transfers between devices  93.5 us (37%)
  Pallas kernels  63 us (25%)
  starting transfers between devices  58.1 us (23%)
  blocking collectives  13.6 us (5%)
  other arithmetic  13.4 us (5%)
  local copies, waits for them, and re-layouts  8.72 us (3%)
    ppermute x9, waiting for transfers between devices, go_out(): return lax.ppermute(value, 'band', pairs)  47.8 us
    ppermute x19, waiting for transfers between devices, swap(): return lax.ppermute(value, 'band', pairs)  45.7 us
    ppermute x19, starting transfers between devices, swap(): return lax.ppermute(value, 'band', pairs)  26 us
    ppermute x9, starting transfers between devices, go_out(): return lax.ppermute(value, 'band', pairs)  21.4 us
    pallas_call x3, Pallas kernels, far_terms(): pl.pallas_call(functools.partial(far_kernel, starts[block]), in_specs=[sm...  14.5 us
    all_to_all x1, blocking collectives, shards(): lax.all_to_all(wanted, 'band', split_axis=0, concat_axis=0, tiled=True)  13.6 us
    pallas_call x1, Pallas kernels, shards(): pl.pallas_call(near_kernel, in_specs=[smem] * 2 + [vmem] * 5, out_specs=v...  11.1 us
    all_to_all x3, starting transfers between devices, go_in(): lax.all_to_all(value, 'band', split_axis=0, concat_axis=0, tiled=True, ax...  10.7 us
  transfers between devices with their start and end apart: 31, of which 10 were waited for; matrix products, arithmetic and copies ran while one was open for 6% of the time, Pallas kernels for 16%

commit v1 on v0

--- a/solution.py
+++ b/solution.py
@@ -11,7 +11,7 @@
 
 EXPS = 3
 OUTER = 4
-BLOCKS = (4, 5, 7)
+BLOCKS = (4, 6, 6)
 section_weight = 0.2
 VMEM_LIMIT = 60 * 1024 * 1024
 
@@ -340,8 +340,20 @@
     lax.fori_loop(0, band_count, operator, 0)
 
 
-def far_kernel(start, ints, flts, base, row, *rest):
-    *parts, out, held, received, diff, summ, sems = rest
+def far_kernel(start, lay, ints, flts, base, row, *rest):
+    if lay:
+        places, *rest = rest
+        pieces, rest = rest[:lay], rest[lay:]
+        *rest, lay_out, held, received, diff, summ, sems, laid, in_sems, out_sems = rest
+        *parts, out = rest
+        pulls = [
+            pltpu.make_async_copy(piece, laid.at[i], in_sems.at[i])
+            for i, piece in enumerate(pieces)
+        ]
+        pushes = lay_copies(places, laid, lay_out, out_sems)
+    else:
+        *parts, out, held, received, diff, summ, sems = rest
+        pulls, pushes = [], []
     block = held.shape[2]
     here = pl.ds(start, block)
     loads = [pltpu.make_async_copy(base.at[:, :, here], held, sems.at[0])]
@@ -351,9 +363,12 @@
         for step, part in enumerate(parts):
             source = part if step else part.at[:, 0]
             loads.append(pltpu.make_async_copy(source, received.at[:, step], sems.at[1 + step]))
-    for load in loads:
+    for load in pulls + loads:
         load.start()
     fill_masks(row, diff, summ, start)
+    for pull, push in zip(pulls, pushes):
+        pull.wait()
+        push.start()
     for load in loads:
         load.wait()
     rows = pl.ds(0, block)
@@ -380,6 +395,8 @@
     lax.fori_loop(0, held.shape[1], operator, 0)
     store = pltpu.make_async_copy(held, out.at[:, :, here], sems.at[0])
     store.start()
+    for push in pushes:
+        push.wait()
     store.wait()
 
 
@@ -405,22 +422,18 @@
     return out
 
 
-def lay_kernel(places, *refs):
-    *pieces, out, sems = refs
-    count = pieces[0].shape[0]
+def lay_copies(places, pieces, out, sems):
+    count = pieces.shape[1]
     copies = []
-    for i, piece in enumerate(pieces):
+    for i in range(pieces.shape[0]):
         core, axis, stream = i // 4, (i // 2) % 2, i % 2
         half = places[0] if core == 0 else 1 - places[0]
         quarter = places[1 + stream] if axis == 0 else 1 - places[1 + stream]
         start = pl.multiple_of((2 * half + quarter) * count, count)
         copies.append(
-            pltpu.make_async_copy(piece, out.at[stream, pl.ds(start, count)], sems.at[i])
+            pltpu.make_async_copy(pieces.at[i], out.at[stream, pl.ds(start, count)], sems.at[i])
         )
-    for copy in copies:
-        copy.start()
-    for copy in copies:
-        copy.wait()
+    return copies
 
 
 def sum_over_band(keep, give, band_size, outer, own_index):
@@ -460,16 +473,7 @@
     pieces = streams + got
     pieces += [swap(piece, 1) for piece in pieces]
     places = jnp.stack([flag[0]] + [flag[b] for b in use]).astype(jnp.int32)
-    count, width = pieces[0].shape
-    return pl.pallas_call(
-        lay_kernel,
-        in_specs=[smem] + [vmem] * 8,
-        out_specs=hbm,
-        out_shape=jax.ShapeDtypeStruct((2, 4 * count, width), jnp.float32),
-        scratch_shapes=[pltpu.SemaphoreType.DMA((8,))],
-        compiler_params=pltpu.CompilerParams(vmem_limit_bytes=VMEM_LIMIT),
-        name="lay",
-    )(places, *pieces)
+    return places, pieces
 
 
 def shards(
@@ -629,8 +633,9 @@
         row,
     )
     flat = (2, -1, size)
-    k_low = sum_over_band(keep.reshape(flat), give.reshape(flat), band_size, outer, own_index)
-    k_low = k_low.reshape(rho_low.shape)
+    places, pieces = sum_over_band(
+        keep.reshape(flat), give.reshape(flat), band_size, outer, own_index
+    )
 
     base = pl.pallas_call(
         own_kernel,
@@ -641,21 +646,36 @@
         name="own",
     )(flts, y_band, hamiltonian)
 
-    def far_terms(k_band, block):
+    def far_terms(k_band, block, pieces=()):
         height = heights[block]
         parts = received[block]
+        out_specs, out_shape = hbm, jax.ShapeDtypeStruct((2, band_count, size, size), f32)
+        scratch = [
+            pltpu.VMEM((2, band_count, height, size), f32),
+            pltpu.VMEM((inner, outer, 2, height, size), f32),
+            pltpu.VMEM((sites, height, size), f32),
+            pltpu.VMEM((sites, height, size), f32),
+            pltpu.SemaphoreType.DMA((1 + len(parts),)),
+        ]
+        lay = []
+        if pieces:
+            lay = [places, *pieces]
+            out_specs = [hbm, hbm]
+            out_shape = [out_shape, jax.ShapeDtypeStruct((2, low_count * size, size), f32)]
+            scratch.append(pltpu.VMEM((len(pieces),) + pieces[0].shape, f32))
+            scratch += [pltpu.SemaphoreType.DMA((len(pieces),))] * 2
         return pl.pallas_call(
-            functools.partial(far_kernel, starts[block]),
-            in_specs=[smem] * 2 + [hbm, vmem] + [hbm] * len(parts),
-            out_specs=hbm,
-            out_shape=jax.ShapeDtypeStruct((2, band_count, size, size), f32),
-            scratch_shapes=[pltpu.VMEM((2, band_count, height, size), f32)]
-            + [pltpu.VMEM((inner, outer, 2, height, size), f32)]
-            + [pltpu.VMEM((sites, height, size), f32)] * 2
-            + [pltpu.SemaphoreType.DMA((1 + len(parts),))],
+            functools.partial(far_kernel, starts[block], len(pieces)),
+            in_specs=[smem] * 2
+            + [hbm, vmem]
+            + ([smem] + [hbm] * len(pieces) if pieces else [])
+            + [hbm] * len(parts),
+            out_specs=out_specs,
+            out_shape=out_shape,
+            scratch_shapes=scratch,
             input_output_aliases={2: 0},
             compiler_params=params(),
-        )(ints_flat, flts_flat, k_band, row, *parts)
+        )(ints_flat, flts_flat, k_band, row, *lay, *parts)
 
     k_band = base
     for block in range(last):
@@ -670,7 +690,8 @@
         compiler_params=params(),
         name="near",
     )(ints_flat, flts_flat, y_band, rho_low, kprev_low, k_band, row)
-    k_band = far_terms(k_band, last)
+    k_band, k_low = far_terms(k_band, last, pieces)
+    k_low = k_low.reshape(rho_low.shape)
     return (k_low, k_band)
 
 

time: 253 us -> 256 us (1.012)
  starting transfers between devices: 58.1 us -> 62.8 us
    ppermute x9, waiting for transfers between devices: 47.8 us -> 32.1 us  [go_out(): return lax.ppermute(value, 'band', pairs)]
    ppermute x19, waiting for transfers between devices: 45.7 us -> 60.7 us  [swap(): return lax.ppermute(value, 'band', pairs)]
    ppermute x19, starting transfers between devices: 26 us -> 29.9 us  [swap(): return lax.ppermute(value, 'band', pairs)]
    pallas_call x4 -> x3, Pallas kernels: 18.7 us -> 17.2 us  [far_terms(): pl.pallas_call(functools.partial(far_kernel, starts[block], len(pieces)),...]
  transfers between devices with their start and end apart: 31 -> 31, of which waited for: 10 -> 9; matrix products, arithmetic and copies ran while one was open for 6% -> 6% of each run, Pallas kernels for 16% -> 14%
where the time goes in v1:
time: 256 us; the launch traced here: 255 us
  waiting for transfers between devices  92.8 us (36%)
  starting transfers between devices  62.8 us (25%)
  Pallas kernels  61.5 us (24%)
  other arithmetic  14 us (5%)
  blocking collectives  13.5 us (5%)
  local copies, waits for them, and re-layouts  9.44 us (4%)
    ppermute x19, waiting for transfers between devices, swap(): return lax.ppermute(value, 'band', pairs)  60.7 us
    ppermute x9, waiting for transfers between devices, go_out(): return lax.ppermute(value, 'band', pairs)  32.1 us
    ppermute x19, starting transfers between devices, swap(): return lax.ppermute(value, 'band', pairs)  29.9 us
    ppermute x9, starting transfers between devices, go_out(): return lax.ppermute(value, 'band', pairs)  22.1 us
    pallas_call x3, Pallas kernels, far_terms(): pl.pallas_call(functools.partial(far_kernel, starts[block], len(pieces)),...  17.2 us
    all_to_all x1, blocking collectives, shards(): lax.all_to_all(wanted, 'band', split_axis=0, concat_axis=0, tiled=True)  13.5 us
    pallas_call x1, Pallas kernels, shards(): pl.pallas_call(near_kernel, in_specs=[smem] * 2 + [vmem] * 5, out_specs=v...  11.1 us
    all_to_all x3, starting transfers between devices, go_in(): lax.all_to_all(value, 'band', split_axis=0, concat_axis=0, tiled=True, ax...  10.7 us
  transfers between devices with their start and end apart: 31, of which 9 were waited for; matrix products, arithmetic and copies ran while one was open for 6% of the time, Pallas kernels for 14%

profile of v1, /device:TPU:0, one launch (start us, length us, event | category | flops | bytes accessed | tf_op | source)
XLA Modules:
  0.0 255.0 jit_solution(7984934978803827329)
XLA Ops:
  2.5 3.8 %advance.1.y_band.refs_3_ = f32[16,2,128,128]{3,2,1,0:T(8,128)} custom-call(f32[2,16,128,128]{3,2,1,0:T(8,128)} %rho.1, f32[2,16,128,128]{3,2,1,0:T(8,128)} %kprev.1), custom_call_target="tpu_custom_call" | custom-call | tf_op jit(solution)/shard_map/advance/pallas_call | solution.py:517
  6.3 6.2 %prep.1 = (s32[8,16,16]{2,1,0:T(8,128)}, f32[7,16,16]{2,1,0:T(8,128)}) custom-call(s32[3]{0:T(128)} %pad_add_fusion.own, s32[16,16]{1,0:T(8,128)} %src.1, s32[16,16]{1,0:T(8,128)} %mode.1, s32[16,16]{1,0:T(8,128)} %direction.1, s32[16,72]{1,0:T(8,128)} %occ.1, f32[1,72]{1,0:T(1,128)} %bitcast.64, f32[1,72]{1,0:T(1,128)} %get-tuple-element.47.cos, ...), custom_call_target="tpu_custom_call" | custom-call | tf_op jit(solution)/shard_map/prep/pallas_call | solution.py:571
  12.5 7.4 %low.1 = (f32[2,16,128,128]{3,2,1,0:T(8,128)}, f32[2,16,128,128]{3,2,1,0:T(8,128)}) custom-call(s32[1]{0:T(128)S(6)} %min.3.ops, s32[1]{0:T(128)} %bitcast.18.refs_0_, s32[8,16,16]{2,1,0:T(8,128)} %get-tuple-element.17.refs_1_, f32[7,16,16]{2,1,0:T(8,128)} %get-tuple-element.18.flts.refs_2_, f32[16,2,128,128]{3,2,1,0:T(8,128)} %advance.1.y_band.refs_3_, ...), custom_call_target="tpu_custom_call" | custom-call | tf_op jit(solution)/shard_map/low/pallas_call | solution.py:604
  20.4 4.0 %collective-permute-done.6 = f32[2,2048,128]{2,1,0:T(8,128)S(1)} collective-permute-done((f32[2,2048,128]{2,1,0:T(8,128)}, f32[2,2048,128]{2,1,0:T(8,128)S(1)}, u32[]{:S(2)}, u32[]{:S(2)}) %collective-permute-start.6) | collective-permute-done | bytes 2097184 | tf_op jit(solution)/shard_map/ppermute | solution.py:449
  30.5 13.5 %all_to_all.20.asked = s32[32,1,128]{2,1,0:T(1,128)} all-to-all(s32[32,1,128]{2,1,0:T(1,128)S(1)} %broadcast_in_dim.40), channel_id=1, replica_groups=mesh['band'=32] {'band'}, dimensions={0} | all-to-all | bytes 32768 | tf_op jit(solution)/shard_map/all_to_all | solution.py:510
  53.2 7.5 %collective-permute-done = f32[8,2,32,128]{3,2,1,0:T(8,128)S(1)} collective-permute-done((f32[8,2,32,128]{3,2,1,0:T(8,128)}, f32[8,2,32,128]{3,2,1,0:T(8,128)S(1)}, u32[]{:S(2)}, u32[]{:S(2)}) %collective-permute-start) | collective-permute-done | bytes 262176 | tf_op jit(solution)/shard_map/ppermute | solution.py:555
  60.7 9.5 %collective-permute-done.1 = f32[8,2,32,128]{3,2,1,0:T(8,128)S(1)} collective-permute-done((f32[8,2,32,128]{3,2,1,0:T(8,128)}, f32[8,2,32,128]{3,2,1,0:T(8,128)S(1)}, u32[]{:S(2)}, u32[]{:S(2)}) %collective-permute-start.1) | collective-permute-done | bytes 262176 | tf_op jit(solution)/shard_map/ppermute | solution.py:555
  72.2 3.6 %all-to-all-start.1 = ((f32[8,4,2,32,128]{4,3,2,1,0:T(8,128)}), f32[8,4,2,32,128]{4,3,2,1,0:T(8,128)S(1)}, u32[]{:S(2)}, u32[]{:S(2)}) async-start(f32[8,4,2,32,128]{4,3,2,1,0:T(8,128)} %pad_maximum_fusion.1), calls=%async_computation.1 | async-start | bytes 2097152 | tf_op jit(solution)/shard_map/all_to_all | solution.py:558
  81.6 4.5 %shard_map.151 = (f32[8,2,48,128]{3,2,1,0:T(8,128)}, f32[8,2,48,128]{3,2,1,0:T(8,128)}, f32[8,2,48,128]{3,2,1,0:T(8,128)}, f32[8,2,48,128]{3,2,1,0:T(8,128)}, f32[8,4,2,48,128]{4,3,2,1,0:T(8,128)}) custom-call(s32[3]{0:T(128)} %pad_add_fusion.own, s32[32,1,128]{2,1,0:T(1,128)} %all_to_all.20.asked, f32[16,2,128,128]{3,2,1,0:T(8,128)} %advance.1.y_band.refs_3_), custom_call_target="tpu_custom_call" | custom-call | tf_op jit(solution)/shard_map/pallas_call | solution.py:534
  86.2 9.6 %collective-permute-done.8 = f32[512,128]{1,0:T(8,128)S(1)} collective-permute-done((f32[512,128]{1,0:T(8,128)S(1)}, f32[512,128]{1,0:T(8,128)S(1)}, u32[]{:S(2)}, u32[]{:S(2)}) %collective-permute-start.8) | collective-permute-done | bytes 262176 | tf_op jit(solution)/shard_map/ppermute | solution.py:449
  96.9 3.6 %all-to-all-start.3 = ((f32[8,4,2,48,128]{4,3,2,1,0:T(8,128)}), f32[8,4,2,48,128]{4,3,2,1,0:T(8,128)S(1)}, u32[]{:S(2)}, u32[]{:S(2)}) async-start(f32[8,4,2,48,128]{4,3,2,1,0:T(8,128)} %get-tuple-element.29), calls=%async_computation.3 | async-start | bytes 3145728 | tf_op jit(solution)/shard_map/all_to_all | solution.py:558
  100.5 4.9 %collective-permute-start.11 = (f32[2,128,128]{2,1,0:T(8,128)S(1)}, f32[2,128,128]{2,1,0:T(8,128)S(1)}, u32[]{:S(2)}, u32[]{:S(2)}) collective-permute-start(f32[2,128,128]{2,1,0:T(8,128)S(1)} %get-tuple-element.41), channel_id=1, source_target_pairs={{0,8},{1,9},{2,10},{3,11},{4,12},{5,13},{6,14},{7,15},{8,0},{9,1},... | collective-permute-start | bytes 393224 | tf_op jit(solution)/shard_map/ppermute | solution.py:449
  108.1 3.5 %collective-permute-done.11 = f32[2,128,128]{2,1,0:T(8,128)S(1)} collective-permute-done((f32[2,128,128]{2,1,0:T(8,128)S(1)}, f32[2,128,128]{2,1,0:T(8,128)S(1)}, u32[]{:S(2)}, u32[]{:S(2)}) %collective-permute-start.11) | collective-permute-done | bytes 131104 | tf_op jit(solution)/shard_map/ppermute | solution.py:449
  111.6 6.7 %collective-permute-done.12 = f32[2,128,128]{2,1,0:T(8,128)S(1)} collective-permute-done((f32[2,128,128]{2,1,0:T(8,128)S(1)}, f32[2,128,128]{2,1,0:T(8,128)S(1)}, u32[]{:S(2)}, u32[]{:S(2)}) %collective-permute-start.12) | collective-permute-done | bytes 131104 | tf_op jit(solution)/shard_map/ppermute | solution.py:449
  129.8 27.5 %collective-permute-done.16 = f32[2,128,128]{2,1,0:T(8,128)S(1)} collective-permute-done((f32[2,128,128]{2,1,0:T(8,128)S(1)}, f32[2,128,128]{2,1,0:T(8,128)S(1)}, u32[]{:S(2)}, u32[]{:S(2)}) %collective-permute-start.16) | collective-permute-done | bytes 131104 | tf_op jit(solution)/shard_map/ppermute | solution.py:449
  163.7 3.6 %all-to-all-start.2 = ((f32[8,4,2,48,128]{4,3,2,1,0:T(8,128)}), f32[8,4,2,48,128]{4,3,2,1,0:T(8,128)S(1)}, u32[]{:S(2)}, u32[]{:S(2)}) async-start(f32[8,4,2,48,128]{4,3,2,1,0:T(8,128)} %pad_maximum_fusion), calls=%async_computation.2 | async-start | bytes 3145728 | tf_op jit(solution)/shard_map/all_to_all | solution.py:558
  176.5 12.3 %collective-permute-start.26 = (f32[8,2,48,128]{3,2,1,0:T(8,128)S(1)}, f32[8,2,48,128]{3,2,1,0:T(8,128)}, u32[]{:S(2)}, u32[]{:S(2)}) collective-permute-start(f32[8,2,48,128]{3,2,1,0:T(8,128)S(1)} %get-tuple-element.37), channel_id=1, source_target_pairs={{0,16},{1,17},{2,18},{3,19},{4,20},{5,21},{6,22},{7,23},{8,24},{9,... | collective-permute-start | bytes 1179656 | tf_op jit(solution)/shard_map/ppermute | solution.py:555
  189.3 9.4 %collective-permute-done.19.rest_3_ = f32[1024,128]{1,0:T(8,128)} collective-permute-done((f32[1024,128]{1,0:T(8,128)}, f32[1024,128]{1,0:T(8,128)}, u32[]{:S(2)}, u32[]{:S(2)}) %collective-permute-start.19) | collective-permute-done | bytes 524320 | tf_op jit(solution)/shard_map/ppermute | solution.py:449
  199.2 15.1 %collective-permute-done.26.rest_11_ = f32[8,2,48,128]{3,2,1,0:T(8,128)} collective-permute-done((f32[8,2,48,128]{3,2,1,0:T(8,128)S(1)}, f32[8,2,48,128]{3,2,1,0:T(8,128)}, u32[]{:S(2)}, u32[]{:S(2)}) %collective-permute-start.26) | collective-permute-done | bytes 393248 | tf_op jit(solution)/shard_map/ppermute | solution.py:555
  215.7 8.0 %own.1.base = f32[2,16,128,128]{3,2,1,0:T(8,128)} custom-call(f32[7,16,16]{2,1,0:T(8,128)} %get-tuple-element.18.flts.refs_2_, f32[16,2,128,128]{3,2,1,0:T(8,128)} %advance.1.y_band.refs_3_, f32[2,128,128]{2,1,0:T(8,128)} %refs_8_.1), custom_call_target="tpu_custom_call" | custom-call | tf_op jit(solution)/shard_map/own/pallas_call | solution.py:640
  224.3 4.4 %shard_map.150.base = f32[2,16,128,128]{3,2,1,0:T(8,128)} custom-call(s32[8,256]{1,0:T(8,128)} %reshape.48.ints, f32[7,256]{1,0:T(8,128)} %reshape.49.flts, f32[2,16,128,128]{3,2,1,0:T(8,128)} %own.1.base, s32[1,128]{1,0:T(1,128)} %bitcast.60, f32[8,4,2,32,128]{4,3,2,1,0:T(8,128)} %copy-done.2), custom_call_target="tpu_custom_call", output_to_operand_aliasing={{}: (2, {})} | custom-call | tf_op jit(solution)/shard_map/pallas_call | solution.py:667
  229.9 5.1 %shard_map.152.base = f32[2,16,128,128]{3,2,1,0:T(8,128)} custom-call(s32[8,256]{1,0:T(8,128)} %reshape.48.ints, f32[7,256]{1,0:T(8,128)} %reshape.49.flts, f32[2,16,128,128]{3,2,1,0:T(8,128)} %shard_map.150.base, s32[1,128]{1,0:T(1,128)} %bitcast.61, f32[8,4,2,48,128]{4,3,2,1,0:T(8,128)} %copy-done.1), custom_call_target="tpu_custom_call", output_to_operand_aliasing={{}: (2, {})} | custom-call | tf_op jit(solution)/shard_map/pallas_call | solution.py:667
  235.0 11.1 %near.1.base = f32[2,16,128,128]{3,2,1,0:T(8,128)} custom-call(s32[8,256]{1,0:T(8,128)} %reshape.48.ints, f32[7,256]{1,0:T(8,128)} %reshape.49.flts, f32[16,2,128,128]{3,2,1,0:T(8,128)} %advance.1.y_band.refs_3_, f32[2,32,128,128]{3,2,1,0:T(8,128)} %refs_6_.1, f32[2,32,128,128]{3,2,1,0:T(8,128)} %refs_7_.1, f32[2,16,128,128]{3,2,1,0:T(8,128)} %shard_map.152.base, ...), custom_call_target="tpu_custom_call" | custom-call | tf_op jit(solution)/shard_map/near/pallas_call | solution.py:683
  247.3 7.7 %shard_map.153 = (f32[2,16,128,128]{3,2,1,0:T(8,128)}, f32[2,4096,128]{2,1,0:T(8,128)}) custom-call(s32[8,256]{1,0:T(8,128)} %reshape.48.ints, f32[7,256]{1,0:T(8,128)} %reshape.49.flts, f32[2,16,128,128]{3,2,1,0:T(8,128)} %near.1.base, s32[1,128]{1,0:T(1,128)} %bitcast.63, s32[3]{0:T(128)} %pad_add_fusion.1.rest_0_, ...), custom_call_target="tpu_custom_call", output_to_operand_aliasing={{0}: (2, {})} | custom-call | tf_op jit(solution)/shard_map/pallas_call | solution.py:667
  (103 shorter events, 61.7 us)
Async XLA Ops:
  27.1 48.6 %collective-permute-start.7 = (f32[1024,128]{1,0:T(8,128)}, f32[1024,128]{1,0:T(8,128)}, u32[]{:S(2)}, u32[]{:S(2)}) collective-permute-start(f32[1024,128]{1,0:T(8,128)} %dynamic-slice_bitcast_fusion.1), channel_id=1, source_target_pairs={{0,2},{1,3},{2,0},{3,1},{4,6},{5,7},{6,4},{7,5},{8,10},{9,11},{10,... | collective-permute-start | bytes 1572872 | tf_op jit(solution)/shard_map/ppermute | solution.py:449
  47.2 13.4 %collective-permute-start = (f32[8,2,32,128]{3,2,1,0:T(8,128)}, f32[8,2,32,128]{3,2,1,0:T(8,128)S(1)}, u32[]{:S(2)}, u32[]{:S(2)}) collective-permute-start(f32[8,2,32,128]{3,2,1,0:T(8,128)} %get-tuple-element.20), channel_id=1, source_target_pairs={{0,8},{1,9},{2,10},{3,11},{4,12},{5,13},{6,14},{7,15},{8,0},{9,1},... | collective-permute-start | bytes 786440 | tf_op jit(solution)/shard_map/ppermute | solution.py:555
  48.6 21.5 %collective-permute-start.1 = (f32[8,2,32,128]{3,2,1,0:T(8,128)}, f32[8,2,32,128]{3,2,1,0:T(8,128)S(1)}, u32[]{:S(2)}, u32[]{:S(2)}) collective-permute-start(f32[8,2,32,128]{3,2,1,0:T(8,128)} %get-tuple-element.21), channel_id=1, source_target_pairs={{0,16},{1,17},{2,18},{3,19},{4,20},{5,21},{6,22},{7,23},{8,24},{9,... | collective-permute-start | bytes 786440 | tf_op jit(solution)/shard_map/ppermute | solution.py:555
  51.2 19.0 %collective-permute-start.2 = (f32[8,2,32,128]{3,2,1,0:T(8,128)}, f32[8,2,32,128]{3,2,1,0:T(8,128)S(1)}, u32[]{:S(2)}, u32[]{:S(2)}) collective-permute-start(f32[8,2,32,128]{3,2,1,0:T(8,128)} %get-tuple-element.22), channel_id=1, source_target_pairs={{0,24},{1,25},{2,26},{3,27},{4,28},{5,29},{6,30},{7,31},{8,16},{9,... | collective-permute-start | bytes 786440 | tf_op jit(solution)/shard_map/ppermute | solution.py:555
  52.5 26.4 %collective-permute-start.9 = (f32[1024,128]{1,0:T(8,128)}, f32[1024,128]{1,0:T(8,128)}, u32[]{:S(2)}, u32[]{:S(2)}) collective-permute-start(f32[1024,128]{1,0:T(8,128)} %dynamic-slice_bitcast_fusion), channel_id=1, source_target_pairs={{0,4},{1,5},{2,6},{3,7},{4,0},{5,1},{6,2},{7,3},{8,12},{9,13},{10,... | collective-permute-start | bytes 1572872 | tf_op jit(solution)/shard_map/ppermute | solution.py:449
  72.2 23.6 %all-to-all-start.1 = ((f32[8,4,2,32,128]{4,3,2,1,0:T(8,128)}), f32[8,4,2,32,128]{4,3,2,1,0:T(8,128)S(1)}, u32[]{:S(2)}, u32[]{:S(2)}) async-start(f32[8,4,2,32,128]{4,3,2,1,0:T(8,128)} %pad_maximum_fusion.1), calls=%async_computation.1 | async-start | bytes 2097152 | tf_op jit(solution)/shard_map/all_to_all | solution.py:558
  76.9 18.8 %collective-permute-start.8 = (f32[512,128]{1,0:T(8,128)S(1)}, f32[512,128]{1,0:T(8,128)S(1)}, u32[]{:S(2)}, u32[]{:S(2)}) collective-permute-start(f32[512,128]{1,0:T(8,128)S(1)} %constant_dynamic-slice_fusion.1), channel_id=1, source_target_pairs={{0,4},{1,5},{2,6},{3,7},{4,0},{5,1},{6,2},{7,3},{8,12},{9,13},{10,... | collective-permute-start | bytes 786440 | tf_op jit(solution)/shard_map/ppermute | solution.py:449
  80.1 15.7 %collective-permute-start.10 = (f32[512,128]{1,0:T(8,128)S(1)}, f32[512,128]{1,0:T(8,128)S(1)}, u32[]{:S(2)}, u32[]{:S(2)}) collective-permute-start(f32[512,128]{1,0:T(8,128)S(1)} %constant_dynamic-slice_fusion), channel_id=1, source_target_pairs={{0,2},{1,3},{2,0},{3,1},{4,6},{5,7},{6,4},{7,5},{8,10},{9,11},{10,... | collective-permute-start | bytes 786440 | tf_op jit(solution)/shard_map/ppermute | solution.py:449
  96.9 66.8 %all-to-all-start.3 = ((f32[8,4,2,48,128]{4,3,2,1,0:T(8,128)}), f32[8,4,2,48,128]{4,3,2,1,0:T(8,128)S(1)}, u32[]{:S(2)}, u32[]{:S(2)}) async-start(f32[8,4,2,48,128]{4,3,2,1,0:T(8,128)} %get-tuple-element.29), calls=%async_computation.3 | async-start | bytes 3145728 | tf_op jit(solution)/shard_map/all_to_all | solution.py:558
  105.4 12.9 %collective-permute-start.12 = (f32[2,128,128]{2,1,0:T(8,128)S(1)}, f32[2,128,128]{2,1,0:T(8,128)S(1)}, u32[]{:S(2)}, u32[]{:S(2)}) collective-permute-start(f32[2,128,128]{2,1,0:T(8,128)S(1)} %get-tuple-element.42), channel_id=1, source_target_pairs={{0,16},{1,17},{2,18},{3,19},{4,20},{5,21},{6,22},{7,23},{8,24},{9,... | collective-permute-start | bytes 393224 | tf_op jit(solution)/shard_map/ppermute | solution.py:449
  122.3 39.0 %collective-permute-start.3 = (f32[8,2,48,128]{3,2,1,0:T(8,128)}, f32[8,2,48,128]{3,2,1,0:T(8,128)S(1)}, u32[]{:S(2)}, u32[]{:S(2)}) collective-permute-start(f32[8,2,48,128]{3,2,1,0:T(8,128)} %get-tuple-element.24), channel_id=1, source_target_pairs={{0,8},{1,9},{2,10},{3,11},{4,12},{5,13},{6,14},{7,15},{8,0},{9,1},... | collective-permute-start | bytes 1179656 | tf_op jit(solution)/shard_map/ppermute | solution.py:555
  124.2 37.0 %collective-permute-start.4 = (f32[8,2,48,128]{3,2,1,0:T(8,128)}, f32[8,2,48,128]{3,2,1,0:T(8,128)}, u32[]{:S(2)}, u32[]{:S(2)}) collective-permute-start(f32[8,2,48,128]{3,2,1,0:T(8,128)} %get-tuple-element.25), channel_id=1, source_target_pairs={{0,16},{1,17},{2,18},{3,19},{4,20},{5,21},{6,22},{7,23},{8,24},{9,... | collective-permute-start | bytes 1179656 | tf_op jit(solution)/shard_map/ppermute | solution.py:555
  124.2 37.0 %collective-permute-start.5 = (f32[8,2,48,128]{3,2,1,0:T(8,128)}, f32[8,2,48,128]{3,2,1,0:T(8,128)}, u32[]{:S(2)}, u32[]{:S(2)}) collective-permute-start(f32[8,2,48,128]{3,2,1,0:T(8,128)} %get-tuple-element.26), channel_id=1, source_target_pairs={{0,24},{1,25},{2,26},{3,27},{4,28},{5,29},{6,30},{7,31},{8,16},{9,... | collective-permute-start | bytes 1179656 | tf_op jit(solution)/shard_map/ppermute | solution.py:555
  126.6 30.7 %collective-permute-start.16 = (f32[2,128,128]{2,1,0:T(8,128)S(1)}, f32[2,128,128]{2,1,0:T(8,128)S(1)}, u32[]{:S(2)}, u32[]{:S(2)}) collective-permute-start(f32[2,128,128]{2,1,0:T(8,128)S(1)} %get-tuple-element.33), channel_id=1, source_target_pairs={{0,24},{1,25},{2,26},{3,27},{4,28},{5,29},{6,30},{7,31},{8,16},{9,... | collective-permute-start | bytes 393224 | tf_op jit(solution)/shard_map/ppermute | solution.py:449
  163.7 65.1 %all-to-all-start.2 = ((f32[8,4,2,48,128]{4,3,2,1,0:T(8,128)}), f32[8,4,2,48,128]{4,3,2,1,0:T(8,128)S(1)}, u32[]{:S(2)}, u32[]{:S(2)}) async-start(f32[8,4,2,48,128]{4,3,2,1,0:T(8,128)} %pad_maximum_fusion), calls=%async_computation.2 | async-start | bytes 3145728 | tf_op jit(solution)/shard_map/all_to_all | solution.py:558
  169.4 29.3 %collective-permute-start.19 = (f32[1024,128]{1,0:T(8,128)}, f32[1024,128]{1,0:T(8,128)}, u32[]{:S(2)}, u32[]{:S(2)}) collective-permute-start(f32[1024,128]{1,0:T(8,128)} %maximum_select_fusion.rest_1_), channel_id=1, source_target_pairs={{0,2},{1,3},{2,0},{3,1},{4,6},{5,7},{6,4},{7,5},{8,10},{9,11},{10,... | collective-permute-start | bytes 1572872 | tf_op jit(solution)/shard_map/ppermute | solution.py:449
  173.2 25.5 %collective-permute-start.20 = (f32[1024,128]{1,0:T(8,128)}, f32[1024,128]{1,0:T(8,128)}, u32[]{:S(2)}, u32[]{:S(2)}) collective-permute-start(f32[1024,128]{1,0:T(8,128)} %maximum_select_fusion.1.rest_2_), channel_id=1, source_target_pairs={{0,4},{1,5},{2,6},{3,7},{4,0},{5,1},{6,2},{7,3},{8,12},{9,13},{10,... | collective-permute-start | bytes 1572872 | tf_op jit(solution)/shard_map/ppermute | solution.py:449
  175.5 13.3 %collective-permute-start.27 = (f32[8,2,48,128]{3,2,1,0:T(8,128)S(1)}, f32[8,2,48,128]{3,2,1,0:T(8,128)}, u32[]{:S(2)}, u32[]{:S(2)}) collective-permute-start(f32[8,2,48,128]{3,2,1,0:T(8,128)S(1)} %get-tuple-element.36), channel_id=1, source_target_pairs={{0,24},{1,25},{2,26},{3,27},{4,28},{5,29},{6,30},{7,31},{8,16},{9,... | collective-permute-start | bytes 1179656 | tf_op jit(solution)/shard_map/ppermute | solution.py:555
  176.5 37.8 %collective-permute-start.26 = (f32[8,2,48,128]{3,2,1,0:T(8,128)S(1)}, f32[8,2,48,128]{3,2,1,0:T(8,128)}, u32[]{:S(2)}, u32[]{:S(2)}) collective-permute-start(f32[8,2,48,128]{3,2,1,0:T(8,128)S(1)} %get-tuple-element.37), channel_id=1, source_target_pairs={{0,16},{1,17},{2,18},{3,19},{4,20},{5,21},{6,22},{7,23},{8,24},{9,... | collective-permute-start | bytes 1179656 | tf_op jit(solution)/shard_map/ppermute | solution.py:555
  188.8 57.3 %collective-permute-start.21 = (f32[1024,128]{1,0:T(8,128)}, f32[1024,128]{1,0:T(8,128)S(1)}, u32[]{:S(2)}, u32[]{:S(2)}) collective-permute-start(f32[1024,128]{1,0:T(8,128)} %maximum_select_fusion.rest_1_), channel_id=1, source_target_pairs={{0,1},{1,0},{2,3},{3,2},{4,5},{5,4},{6,7},{7,6},{8,9},{9,8},{10,11... | collective-permute-start | bytes 1572872 | tf_op jit(solution)/shard_map/ppermute | solution.py:449
  188.8 57.3 %collective-permute-start.22 = (f32[1024,128]{1,0:T(8,128)}, f32[1024,128]{1,0:T(8,128)S(1)}, u32[]{:S(2)}, u32[]{:S(2)}) collective-permute-start(f32[1024,128]{1,0:T(8,128)} %maximum_select_fusion.1.rest_2_), channel_id=1, source_target_pairs={{0,1},{1,0},{2,3},{3,2},{4,5},{5,4},{6,7},{7,6},{8,9},{9,8},{10,11... | collective-permute-start | bytes 1572872 | tf_op jit(solution)/shard_map/ppermute | solution.py:449
  198.7 47.5 %collective-permute-start.23 = (f32[1024,128]{1,0:T(8,128)}, f32[1024,128]{1,0:T(8,128)S(1)}, u32[]{:S(2)}, u32[]{:S(2)}) collective-permute-start(f32[1024,128]{1,0:T(8,128)} %collective-permute-done.19.rest_3_), channel_id=1, source_target_pairs={{0,1},{1,0},{2,3},{3,2},{4,5},{5,4},{6,7},{7,6},{8,9},{9,8},{10,11... | collective-permute-start | bytes 1572872 | tf_op jit(solution)/shard_map/ppermute | solution.py:449
  198.7 47.5 %collective-permute-start.24 = (f32[1024,128]{1,0:T(8,128)}, f32[1024,128]{1,0:T(8,128)}, u32[]{:S(2)}, u32[]{:S(2)}) collective-permute-start(f32[1024,128]{1,0:T(8,128)} %collective-permute-done.20.rest_4_), channel_id=1, source_target_pairs={{0,1},{1,0},{2,3},{3,2},{4,5},{5,4},{6,7},{7,6},{8,9},{9,8},{10,11... | collective-permute-start | bytes 1572872 | tf_op jit(solution)/shard_map/ppermute | solution.py:449
  214.3 31.8 %collective-permute-start.25 = (f32[8,2,48,128]{3,2,1,0:T(8,128)}, f32[8,2,48,128]{3,2,1,0:T(8,128)}, u32[]{:S(2)}, u32[]{:S(2)}) collective-permute-start(f32[8,2,48,128]{3,2,1,0:T(8,128)} %get-tuple-element.38), channel_id=1, source_target_pairs={{0,8},{1,9},{2,10},{3,11},{4,12},{5,13},{6,14},{7,15},{8,0},{9,1},... | collective-permute-start | bytes 1179656 | tf_op jit(solution)/shard_map/ppermute | solution.py:555
  (19 other events, 263.2 us)
